TPU v7x, 32 devices: a whole 2x2x4 slice. The times are simulated.
32 devices in a mesh: rev: 8 (over y, x, core), row: 4 (over z).
Axes of the slice: x: 2, y: 2, z: 4, core: 2. Of those that a mesh axis runs over, the one named last changes fastest.
Arguments:
- fields: bfloat16 [8, 16, 1024, 1024], P('rev', None, 'row'), may hold values from -6 to 6
- out_grads: bfloat16 [8, 16, 1024, 1024], P('rev', None, 'row'), may hold values from -6 to 6
- partner: int32 [8], replicated, may hold values from 0 to 7, as said below
- kept_blocks: int32 [8], replicated, may hold values from 1 to 8
- weight_in: float32 [1, 2, 32, 16], replicated, may hold values from -0.75 to 0.75
- bias_in: float32 [1, 2, 16], replicated, may hold values from -3 to 3
- weight_out: float32 [1, 2, 16, 16], replicated, may hold values from -1 to 1
Outputs:
- field_grads: bfloat16 [8, 16, 1024, 1024], P('rev', None, 'row')
- grad_weight_in: float32 [1, 2, 32, 16], replicated
- grad_bias_in: float32 [1, 2, 16], replicated
- grad_weight_out: float32 [1, 2, 16, 16], replicated
- grad_bias_out: float32 [1, 2, 16], replicated
Inputs may be any that keep to these rules, and one draw needn't show every extreme that they name: partner[partner[r]] = r and partner[r] != r for every revision r; some revision r has partner[r] = (r + 4) mod 8.
All inputs are finite; a program needn't handle non-finite values.
Results may differ from a plain program's by a relative error of at most 0.01.
Values may be sent and summed in bfloat16 or wider, within the bound.
A program may use at most 128 MiB of HBM per device.

v0:
```python
import math
import jax
import jax.numpy as jnp
from jax import lax
from jax.sharding import PartitionSpec as P

NH = 1024
NW = 1024
KX = 128
MB = 16
KY = 256
HIGHEST = lax.Precision.HIGHEST


def column_tables(n_cols, n_keep):
    col_index = jnp.arange(n_cols, dtype=jnp.int32)[:, None]
    freq_index = jnp.arange(n_keep, dtype=jnp.int32)[None, :]
    phases = col_index * freq_index % n_cols
    angles = phases.astype(jnp.float32) * (2.0 * math.pi / n_cols)
    return (jnp.cos(angles).astype(jnp.bfloat16), jnp.sin(angles).astype(jnp.bfloat16))


def row_tables(n_rows, n_keep):
    row_index = jnp.arange(n_rows, dtype=jnp.int32)[None, :]
    slot_index = jnp.arange(n_keep, dtype=jnp.int32)
    signed = jnp.where(slot_index < n_keep // 2, slot_index, slot_index - n_keep + n_rows)
    phases = signed[:, None] * row_index % n_rows
    angles = phases.astype(jnp.float32) * (2.0 * math.pi / n_rows)
    return (jnp.cos(angles).astype(jnp.bfloat16), jnp.sin(angles).astype(jnp.bfloat16))


def keep_mask(kept_count, col_index, n_keep):
    slot_index = jnp.arange(n_keep, dtype=jnp.int32)
    row_extent = jnp.where(slot_index < n_keep // 2, slot_index, n_keep - slot_index)
    extent = jnp.maximum(col_index[:, None], row_extent[None, :])
    return (extent < kept_count * MB).astype(jnp.float32)


def complex_layer(weights, biases, real_part, imag_part):

    def mixing(matrix, values):
        return jnp.einsum("bio,bipq->bopq", matrix, values, precision=HIGHEST)

    weight_real = weights[:, 0]
    weight_imag = weights[:, 1]
    out_real = (
        mixing(weight_real, real_part)
        - mixing(weight_imag, imag_part)
        + biases[:, 0, :, None, None]
    )
    out_imag = (
        mixing(weight_imag, real_part)
        + mixing(weight_real, imag_part)
        + biases[:, 1, :, None, None]
    )
    return (out_real, out_imag)


def spectral_mlp(params, own_spec, other_spec):
    weight_in, bias_in, weight_out, bias_out = params
    blocks = weight_in.shape[0]
    block_width = own_spec.shape[1] // blocks
    trailing = own_spec.shape[2:]

    def split_blocks(spectrum):
        return spectrum.reshape((2, blocks, block_width) + trailing)

    joined = jnp.concatenate([split_blocks(own_spec), split_blocks(other_spec)], axis=2)
    hidden_real, hidden_imag = complex_layer(weight_in, bias_in, joined[0], joined[1])
    hidden_real = jax.nn.gelu(hidden_real, approximate=True)
    hidden_imag = jax.nn.gelu(hidden_imag, approximate=True)
    out_real, out_imag = complex_layer(weight_out, bias_out, hidden_real, hidden_imag)
    return jnp.stack([out_real, out_imag]).reshape((2, blocks * block_width) + trailing)


def mlp_backward(params, own_spec, other_spec, cotangent):
    unused, pullback = jax.vjp(spectral_mlp, params, own_spec, other_spec)
    return pullback(cotangent)


def column_pass(field, col_cos, col_sin):
    channels, n_rows, n_cols = field.shape
    flattened = field.reshape(channels * n_rows, n_cols)
    real_cols = jnp.dot(flattened, col_cos, preferred_element_type=jnp.float32)
    imag_cols = -jnp.dot(flattened, col_sin, preferred_element_type=jnp.float32)
    return jnp.stack([real_cols, imag_cols]).astype(jnp.bfloat16).reshape(2, channels, n_rows, -1)


def row_spectrum(column_spec, row_cos, row_sin):
    with_cos = jnp.einsum("schk,jh->sckj", column_spec, row_cos, preferred_element_type=jnp.float32)
    with_sin = jnp.einsum("schk,jh->sckj", column_spec, row_sin, preferred_element_type=jnp.float32)
    real_part = with_cos[0] + with_sin[1]
    imag_part = with_cos[1] - with_sin[0]
    return jnp.stack([real_part, imag_part]) * (1.0 / math.sqrt(NH * NW))


def inverse_rows(total, row_cos, row_sin):
    with_cos = jnp.einsum("sckj,jh->schk", total, row_cos, preferred_element_type=jnp.float32)
    with_sin = jnp.einsum("sckj,jh->schk", total, row_sin, preferred_element_type=jnp.float32)
    real_part = with_cos[0] - with_sin[1]
    imag_part = with_sin[0] + with_cos[1]
    return jnp.stack([real_part, imag_part]).astype(jnp.bfloat16)


def inverse_cols(rows_spec, col_cos, col_sin):
    channels, n_rows, n_keep = rows_spec.shape[1:]
    real_rows = rows_spec[0].reshape(channels * n_rows, n_keep)
    imag_rows = rows_spec[1].reshape(channels * n_rows, n_keep)
    result_real = jnp.einsum("hk,wk->hw", real_rows, col_cos, preferred_element_type=jnp.float32)
    result_imag = jnp.einsum("hk,wk->hw", imag_rows, col_sin, preferred_element_type=jnp.float32)
    field = (result_real - result_imag) * (1.0 / math.sqrt(NH * NW))
    return field.astype(jnp.bfloat16).reshape(channels, n_rows, -1)


def local(fields, out_grads, partner, kept_blocks, weight_in, bias_in, weight_out):
    col_cos, col_sin = column_tables(NW, KX)
    row_cos, row_sin = row_tables(NH, KY)
    own_rev = lax.axis_index("rev")
    row_rank = lax.axis_index("row")
    local_cols = KX // lax.axis_size("row")
    field_cols = column_pass(fields[0], col_cos, col_sin)
    grad_cols = column_pass(out_grads[0], col_cos, col_sin)
    spectra = row_spectrum(
        lax.all_to_all(field_cols, "row", split_axis=3, concat_axis=2, tiled=True), row_cos, row_sin
    )
    grad_spec = row_spectrum(
        lax.all_to_all(grad_cols, "row", split_axis=3, concat_axis=2, tiled=True), row_cos, row_sin
    )

    def route(spectrum):
        target = partner[own_rev]
        slot_array = jnp.zeros((lax.axis_size("rev"),) + spectrum.shape, spectrum.dtype)
        slot_array = lax.dynamic_update_index_in_dim(slot_array, spectrum, target, 0)
        received = lax.all_to_all(slot_array, "rev", split_axis=0, concat_axis=0, tiled=True)
        return lax.dynamic_index_in_dim(received, target, 0, keepdims=False)

    partner_spec = route(spectra.astype(jnp.bfloat16)).astype(jnp.float32)
    col_index = row_rank * local_cols + jnp.arange(local_cols, dtype=jnp.int32)
    keep_local = keep_mask(kept_blocks[own_rev], col_index, KY)
    params = (weight_in, bias_in, weight_out, jnp.zeros_like(bias_in))
    param_grads, own_grads, other_grads = mlp_backward(
        params, spectra, partner_spec, grad_spec * keep_local[None, None]
    )
    returned = route(other_grads.astype(jnp.bfloat16)).astype(jnp.float32)
    total = (own_grads + returned).astype(jnp.bfloat16)
    rows_spec = inverse_rows(total, row_cos, row_sin)
    field_grads = inverse_cols(
        lax.all_to_all(rows_spec, "row", split_axis=2, concat_axis=3, tiled=True), col_cos, col_sin
    )
    summed = lax.psum(
        (param_grads[0], param_grads[1], param_grads[2], param_grads[3]), ("rev", "row")
    )
    grad_scale = 1.0 / math.sqrt(lax.axis_size("rev") * KX * KY)
    return (
        field_grads[None],
        summed[0] * grad_scale,
        summed[1] * grad_scale,
        summed[2] * grad_scale,
        summed[3] * grad_scale,
    )


def solution(mesh):
    placed = (P("rev", None, "row", None), P("rev", None, "row", None), P(), P(), P(), P(), P())
    return jax.shard_map(
        local,
        mesh=mesh,
        in_specs=placed,
        out_specs=(P("rev", None, "row", None), P(), P(), P(), P()),
        check_vma=False,
    )
```

profile of v0, /device:TPU:0, one launch (start us, length us, event | category | flops | bytes accessed | tf_op | source)
XLA Modules:
  0.0 385.1 jit_solution(9175087213200670544)
XLA Ops:
  0.6 8.1 %fusion.1 = bf16[128,4096]{1,0:T(8,128)(2,1)S(1)} fusion(bf16[4096,1024]{1,0:T(8,128)(2,1)} %bitcast.364), kind=kOutput, calls=%fused_computation.4 | convolution fusion | flops 1076756480 | bytes 9437184 | tf_op jit(solution)/shard_map/dot_general | solution.py:85
  8.8 4.6 %convolution_convert_fusion = bf16[128,4096]{1,0:T(8,128)(2,1)S(1)} fusion(bf16[4096,1024]{1,0:T(8,128)(2,1)S(1)} %bitcast.365), kind=kOutput, calls=%fused_computation.5 | convolution fusion | flops 1076232192 | bytes 9437184 | tf_op jit(solution)/shard_map/dot_general | solution.py:84
  15.4 6.5 %all-to-all-start.1 = ((bf16[2,16,256,128]{2,1,0,3:T(8,128)(2,1)}), bf16[2,16,256,128]{2,1,0,3:T(8,128)(2,1)S(1)}, u32[]{:S(2)}, u32[]{:S(2)}) async-start(bf16[2,16,256,128]{2,1,0,3:T(8,128)(2,1)} %pad_maximum_fusion.1), calls=%async_computation.1 | async-start | bytes 4194304 | tf_op jit(solution)/shard_map/all_to_all | solution.py:124
  21.9 8.0 %fusion = bf16[128,4096]{1,0:T(8,128)(2,1)S(1)} fusion(bf16[4096,1024]{1,0:T(8,128)(2,1)} %bitcast.366), kind=kOutput, calls=%fused_computation.3 | convolution fusion | flops 1076756480 | bytes 9437184 | tf_op jit(solution)/shard_map/dot_general | solution.py:85
  30.2 8.0 %convolution_convert_fusion.1 = bf16[128,4096]{1,0:T(8,128)(2,1)S(1)} fusion(bf16[4096,1024]{1,0:T(8,128)(2,1)} %bitcast.367), kind=kOutput, calls=%fused_computation.6 | convolution fusion | flops 1076232192 | bytes 9437184 | tf_op jit(solution)/shard_map/dot_general | solution.py:84
  40.0 30.2 %all-to-all-done.1 = bf16[2,16,256,128]{2,1,0,3:T(8,128)(2,1)S(1)} async-done(((bf16[2,16,256,128]{2,1,0,3:T(8,128)(2,1)}), bf16[2,16,256,128]{2,1,0,3:T(8,128)(2,1)S(1)}, u32[]{:S(2)}, u32[]{:S(2)}) %all-to-all-start.1) | async-done | bytes 2097184 | tf_op jit(solution)/shard_map/all_to_all | solution.py:124
  71.4 4.0 %all-to-all-start = ((bf16[2,16,256,128]{2,1,0,3:T(8,128)(2,1)}), bf16[2,16,256,128]{2,1,0,3:T(8,128)(2,1)S(1)}, u32[]{:S(2)}, u32[]{:S(2)}) async-start(bf16[2,16,256,128]{2,1,0,3:T(8,128)(2,1)} %pad_maximum_fusion), calls=%async_computation | async-start | bytes 4194304 | tf_op jit(solution)/shard_map/all_to_all | solution.py:127
  78.0 4.5 %copy.142 = bf16[2,16,256,4,32]{2,3,4,1,0:T(4,128)(2,1)} copy(bf16[2,16,256,4,32]{2,1,0,4,3:T(8,128)(2,1)} %bitcast.346) | data formatting | bytes 4194304 | tf_op jit(solution)/shard_map/all_to_all | solution.py:124
  82.5 4.4 %all_to_all.50 = bf16[2,16,1024,32]{2,3,1,0:T(8,128)(2,1)} reshape(bf16[2,16,4,256,32]{3,2,4,1,0:T(4,128)(2,1)} %bitcast.347) | data formatting | bytes 4194304 | tf_op jit(solution)/shard_map/all_to_all | solution.py:124
  87.0 6.3 %fusion.88 = f32[2,16,32,256]{3,2,1,0:T(8,128)S(1)} fusion(bf16[2,16,1024,32]{2,3,1,0:T(8,128)(2,1)} %all_to_all.50, s32[256]{0:T(256)S(1)} %compare_select_fusion.1), kind=kOutput, calls=%fused_computation.150 | convolution fusion | flops 540803072 | bytes 3146752 | tf_op jit(solution)/shard_map/schk,jh->sckj/dot_general | solution.py:91
  93.2 4.5 %fusion.93 = f32[2,16,32,256]{3,2,1,0:T(8,128)S(1)} fusion(bf16[2,16,1024,32]{2,3,1,0:T(8,128)(2,1)S(1)} %copy-done.4, s32[256]{0:T(256)S(1)} %compare_select_fusion.1), kind=kOutput, calls=%fused_computation.152 | convolution fusion | flops 540803072 | bytes 3146752 | tf_op jit(solution)/shard_map/schk,jh->sckj/dot_general | solution.py:90
  97.9 2.5 broadcast.158.clone
  101.4 21.7 %all-to-all-done = bf16[2,16,256,128]{2,1,0,3:T(8,128)(2,1)S(1)} async-done(((bf16[2,16,256,128]{2,1,0,3:T(8,128)(2,1)}), bf16[2,16,256,128]{2,1,0,3:T(8,128)(2,1)S(1)}, u32[]{:S(2)}, u32[]{:S(2)}) %all-to-all-start) | async-done | bytes 2097184 | tf_op jit(solution)/shard_map/all_to_all | solution.py:127
  123.1 4.6 %all-to-all-start.2 = ((bf16[8,2,16,32,256]{4,3,2,1,0:T(8,128)(2,1)}), bf16[8,2,16,32,256]{4,3,2,1,0:T(8,128)(2,1)}, u32[]{:S(2)}, u32[]{:S(2)}) async-start(bf16[8,2,16,32,256]{4,3,2,1,0:T(8,128)(2,1)} %fusion.62), calls=%async_computation.2 | async-start | bytes 8388608 | tf_op jit(solution)/shard_map/all_to_all | solution.py:134
  129.1 3.0 copy.143
  132.0 3.4 all_to_all.46
  136.5 4.5 %fusion.90 = f32[2,16,32,256]{3,2,1,0:T(8,128)S(1)} fusion(bf16[2,16,1024,32]{2,3,1,0:T(8,128)(2,1)S(1)} %all_to_all.46, s32[256]{0:T(256)S(1)} %compare_select_fusion.1), kind=kOutput, calls=%fused_computation.151 | convolution fusion | flops 540803072 | bytes 3146752 | tf_op jit(solution)/shard_map/schk,jh->sckj/dot_general | solution.py:91
  141.1 4.5 %fusion.95 = f32[2,16,32,256]{3,2,1,0:T(8,128)S(1)} fusion(bf16[2,16,1024,32]{2,3,1,0:T(8,128)(2,1)S(1)} %all_to_all.46, s32[256]{0:T(256)S(1)} %compare_select_fusion.1), kind=kOutput, calls=%fused_computation.153 | convolution fusion | flops 540803072 | bytes 3146752 | tf_op jit(solution)/shard_map/schk,jh->sckj/dot_general | solution.py:90
  148.7 1.7 fusion.108
  150.4 26.4 %all-to-all-done.2 = bf16[8,2,16,32,256]{4,3,2,1,0:T(8,128)(2,1)} async-done(((bf16[8,2,16,32,256]{4,3,2,1,0:T(8,128)(2,1)}), bf16[8,2,16,32,256]{4,3,2,1,0:T(8,128)(2,1)}, u32[]{:S(2)}, u32[]{:S(2)}) %all-to-all-start.2) | async-done | bytes 4194336 | tf_op jit(solution)/shard_map/all_to_all | solution.py:134
  191.0 2.5 fusion.28
  194.1 51.6 %all_to_all.61 = bf16[8,2,16,32,256]{4,3,2,1,0:T(8,128)(2,1)S(1)} all-to-all(bf16[8,2,16,32,256]{4,3,2,1,0:T(8,128)(2,1)S(1)} %fusion.64), channel_id=1, replica_groups=mesh['rev'=8,'row'=4] {'rev'}, dimensions={0} | all-to-all | bytes 8388608 | tf_op jit(solution)/shard_map/all_to_all | solution.py:134
  245.8 4.6 %convolution_bitcast_fusion = f32[2,16,1024,32]{2,3,1,0:T(8,128)S(1)} fusion(bf16[2,16,32,256]{3,2,1,0:T(8,128)(2,1)S(1)} %fusion.22, s32[256]{0:T(256)S(1)} %compare_select_fusion.1), kind=kOutput, calls=%fused_computation.7 | convolution fusion | flops 540803072 | bytes 4719616 | tf_op jit(solution)/shard_map/sckj,jh->schk/dot_general | solution.py:99
  250.4 4.5 %convolution_bitcast_fusion.1 = f32[2,16,1024,32]{2,3,1,0:T(8,128)S(1)} fusion(bf16[2,16,32,256]{3,2,1,0:T(8,128)(2,1)S(1)} %fusion.22, s32[256]{0:T(256)S(1)} %compare_select_fusion.1), kind=kOutput, calls=%fused_computation.8 | convolution fusion | flops 540803072 | bytes 4719616 | tf_op jit(solution)/shard_map/sckj,jh->schk/dot_general | solution.py:98
  257.6 12.5 %copy.77 = bf16[2,16,1024,32]{3,1,0,2:T(8,128)(2,1)} copy(bf16[2,16,1024,32]{2,3,1,0:T(8,128)(2,1)} %pad_maximum_fusion.2) | data formatting | bytes 4194304 | tf_op jit(solution)/shard_map/stack | solution.py:102
  270.1 10.7 %reshape.381 = bf16[4,2,131072]{2,1,0:T(2,128)(2,1)} reshape(bf16[1024,2,16,32]{3,2,1,0:T(8,128)(2,1)} %bitcast.340) | data formatting | bytes 4194304
  280.8 4.4 %all-to-all-start.4 = ((bf16[4,2,131072]{2,1,0:T(2,128)(2,1)}), bf16[4,2,131072]{2,1,0:T(2,128)(2,1)}, u32[]{:S(2)}, u32[]{:S(2)}) async-start(bf16[4,2,131072]{2,1,0:T(2,128)(2,1)} %reshape.381), calls=%async_computation.4 | async-start | bytes 4194304 | tf_op jit(solution)/shard_map/all_to_all | solution.py:148
  295.2 57.3 %all-reduce.10 = (f32[1,2,32,16]{2,3,1,0:T(8,128)S(1)}, f32[1,2,16]{2,1,0:T(2,128)S(1)}, f32[1,2,16,16]{2,3,1,0:T(8,128)S(1)}, f32[1,2,16]{2,1,0:T(2,128)S(1)}) all-reduce(f32[1,2,32,16]{2,3,1,0:T(8,128)S(1)} %pad_add_fusion.2, f32[1,2,16]{2,1,0:T(2,128)S(1)} %pad_add_fusion.4, ...), channel_id=1, replica_groups=mesh['rev'=8,'row'=4] {'rev','row'}, use_global_device_ids=true, to_apply=%region_0.1 | all-reduce | flops 1600 | bytes 12800 | tf_op jit(solution)/shard_map/psum | solution.py:150
  354.4 7.3 %reshape.382 = bf16[1024,2,16,32]{3,2,1,0:T(8,128)(2,1)} reshape(bf16[4,2,131072]{2,1,0:T(2,128)(2,1)} %all-to-all-done.4) | data formatting | bytes 4194304
  361.8 10.9 %copy.78 = bf16[2,16,4,256,32]{3,1,4,2,0:T(8,128)(2,1)S(1)} copy(bf16[2,16,4,256,32]{4,1,0,3,2:T(8,128)(2,1)} %bitcast.341) | data formatting | bytes 4194304 | tf_op jit(solution)/shard_map/all_to_all | solution.py:148
  373.8 4.4 %fusion.110 = f32[4096,1024]{1,0:T(8,128)S(1)} fusion(bf16[4096,128]{0,1:T(8,128)(2,1)S(1)} %bitcast.349), kind=kOutput, calls=%fused_computation.171 | convolution fusion | flops 1075707904 | bytes 17825792 | tf_op jit(solution)/shard_map/hk,wk->hw/dot_general | solution.py:109
  378.2 6.5 %multiply_convert_fusion = bf16[4096,1024]{1,0:T(8,128)(2,1)} fusion(f32[4096,1024]{1,0:T(8,128)S(1)} %fusion.110, bf16[4096,128]{0,1:T(8,128)(2,1)S(1)} %bitcast.343), kind=kOutput, calls=%fused_computation | convolution fusion | flops 1088290816 | bytes 26214400 | tf_op jit(solution)/shard_map/hk,wk->hw/dot_general | solution.py:110
  (99 shorter events, 42.2 us)
Async XLA Ops:
  0.6 8.1 %copy-start.18 = (bf16[1,16,256,1024]{3,2,1,0:T(8,128)(2,1)S(1)}, bf16[1,16,256,1024]{3,2,1,0:T(8,128)(2,1)}, u32[]{:S(2)}) copy-start(bf16[1,16,256,1024]{3,2,1,0:T(8,128)(2,1)} %param.7) | copy-start | bytes 25165828
  15.4 54.7 %all-to-all-start.1 = ((bf16[2,16,256,128]{2,1,0,3:T(8,128)(2,1)}), bf16[2,16,256,128]{2,1,0,3:T(8,128)(2,1)S(1)}, u32[]{:S(2)}, u32[]{:S(2)}) async-start(bf16[2,16,256,128]{2,1,0,3:T(8,128)(2,1)} %pad_maximum_fusion.1), calls=%async_computation.1 | async-start | bytes 4194304 | tf_op jit(solution)/shard_map/all_to_all | solution.py:124
  40.0 35.5 %copy-start.19 = (s32[8]{0:T(128)S(1)}, s32[8]{0:T(128)}, u32[]{:S(2)}) copy-start(s32[8]{0:T(128)} %param.9) | copy-start | bytes 100
  70.1 1.3 copy-start
  71.4 51.7 %all-to-all-start = ((bf16[2,16,256,128]{2,1,0,3:T(8,128)(2,1)}), bf16[2,16,256,128]{2,1,0,3:T(8,128)(2,1)S(1)}, u32[]{:S(2)}, u32[]{:S(2)}) async-start(bf16[2,16,256,128]{2,1,0,3:T(8,128)(2,1)} %pad_maximum_fusion), calls=%async_computation | async-start | bytes 4194304 | tf_op jit(solution)/shard_map/all_to_all | solution.py:127
  87.0 6.3 %copy-start.4 = (bf16[2,16,1024,32]{2,3,1,0:T(8,128)(2,1)S(1)}, bf16[2,16,1024,32]{2,3,1,0:T(8,128)(2,1)}, u32[]{:S(2)}) copy-start(bf16[2,16,1024,32]{2,3,1,0:T(8,128)(2,1)} %all_to_all.50) | copy-start | bytes 6291460
  101.4 26.3 %copy-start.20 = (s32[8]{0:T(128)S(1)}, s32[8]{0:T(128)}, u32[]{:S(2)}) copy-start(s32[8]{0:T(128)} %param.10) | copy-start | bytes 100
  101.4 27.5 %copy-start.17 = (f32[1,2,16]{2,1,0:T(2,128)S(1)}, f32[1,2,16]{2,1,0:T(2,128)}, u32[]{:S(2)}) copy-start(f32[1,2,16]{2,1,0:T(2,128)} %param.12) | copy-start | bytes 388
  123.1 53.7 %all-to-all-start.2 = ((bf16[8,2,16,32,256]{4,3,2,1,0:T(8,128)(2,1)}), bf16[8,2,16,32,256]{4,3,2,1,0:T(8,128)(2,1)}, u32[]{:S(2)}, u32[]{:S(2)}) async-start(bf16[8,2,16,32,256]{4,3,2,1,0:T(8,128)(2,1)} %fusion.62), calls=%async_computation.2 | async-start | bytes 8388608 | tf_op jit(solution)/shard_map/all_to_all | solution.py:134
  145.8 1.2 copy-start.16
  147.0 1.7 copy-start.1
  147.0 30.9 %copy-start.3 = (f32[2,1,16,32,256]{4,3,2,1,0:T(8,128)S(1)}, f32[2,1,16,32,256]{4,3,2,1,0:T(8,128)}, u32[]{:S(2)}) copy-start(f32[2,1,16,32,256]{4,3,2,1,0:T(8,128)} %maximum_multiply_fusion.1) | copy-start | bytes 3145732
  178.0 0.7 copy-start.15
  180.4 2.6 copy-start.5
  180.4 2.6 copy-start.14
  183.0 2.3 copy-start.9
  185.3 2.3 copy-start.7
  185.3 2.3 copy-start.13
  187.6 2.3 copy-start.11
  280.8 73.6 %all-to-all-start.4 = ((bf16[4,2,131072]{2,1,0:T(2,128)(2,1)}), bf16[4,2,131072]{2,1,0:T(2,128)(2,1)}, u32[]{:S(2)}, u32[]{:S(2)}) async-start(bf16[4,2,131072]{2,1,0:T(2,128)(2,1)} %reshape.381), calls=%async_computation.4 | async-start | bytes 4194304 | tf_op jit(solution)/shard_map/all_to_all | solution.py:148
  286.7 4.3 %copy-start.8 = (f32[16,32,256]{2,1,0:T(8,128)S(1)}, f32[16,32,256]{2,1,0:T(8,128)}, u32[]{:S(2)}) copy-start(f32[16,32,256]{2,1,0:T(8,128)} %get-tuple-element.36) | copy-start | bytes 1572868
  286.7 4.3 %copy-start.12 = (f32[32,256,16]{1,2,0:T(8,128)S(1)}, f32[32,256,16]{1,2,0:T(8,128)}, u32[]{:S(2)}) copy-start(f32[32,256,16]{1,2,0:T(8,128)} %copy-done.11) | copy-start | bytes 1572868
  288.1 3.9 %copy-start.6 = (f32[16,32,256]{2,1,0:T(8,128)S(1)}, f32[16,32,256]{2,1,0:T(8,128)}, u32[]{:S(2)}) copy-start(f32[16,32,256]{2,1,0:T(8,128)} %get-tuple-element.37) | copy-start | bytes 1572868
  288.1 3.9 %copy-start.10 = (f32[32,256,16]{1,2,0:T(8,128)S(1)}, f32[32,256,16]{1,2,0:T(8,128)}, u32[]{:S(2)}) copy-start(f32[32,256,16]{1,2,0:T(8,128)} %copy-done.9) | copy-start | bytes 1572868
  289.5 3.5 copy-start.2
where the time goes:
time: 393 us; the launch traced here: 385 us
  blocking collectives  109 us (28%)
  matrix products  93.7 us (24%)
  waiting for transfers between devices  78.3 us (20%)
  local copies, waits for them, and re-layouts  65.6 us (17%)
  starting transfers between devices  19.5 us (5%)
  other arithmetic  14.8 us (4%)
  between operations  4.32 us (1%)
    psum x1, blocking collectives, local(): lax.psum((param_grads[0], param_grads[1], param_grads[2], param_grads[3])...  57.3 us
    all_to_all x1, blocking collectives, route(): lax.all_to_all(slot_array, 'rev', split_axis=0, concat_axis=0, tiled=True)  51.6 us
    all_to_all x1, waiting for transfers between devices, local(): lax.all_to_all(field_cols, 'row', split_axis=3, concat_axis=2, tiled=True)  30.2 us
    all_to_all x1, waiting for transfers between devices, route(): lax.all_to_all(slot_array, 'rev', split_axis=0, concat_axis=0, tiled=True)  26.4 us
    dot_general x20, matrix products, mixing(): return jnp.einsum('bio,bipq->bopq', matrix, values, precision=HIGHEST)  25.2 us
    unnamed x51, local copies, waits for them, and re-layouts  22.5 us
    all_to_all x1, waiting for transfers between devices, local(): lax.all_to_all(grad_cols, 'row', split_axis=3, concat_axis=2, tiled=True)  21.7 us
    dot_general x2, matrix products, column_pass(): imag_cols = -jnp.dot(flattened, col_sin, preferred_element_type=jnp.float32)  16.1 us
  transfers between devices with their start and end apart: 4, of which 3 were waited for; matrix products, arithmetic and copies ran while one was open for 18% of the time, Pallas kernels for 0%

commit v1 on v0

--- a/solution.py
+++ b/solution.py
@@ -148,7 +148,7 @@
         lax.all_to_all(rows_spec, "row", split_axis=2, concat_axis=3, tiled=True), col_cos, col_sin
     )
     summed = lax.psum(
-        (param_grads[0], param_grads[1], param_grads[2], param_grads[3]), ("rev", "row")
+        lax.psum((param_grads[0], param_grads[1], param_grads[2], param_grads[3]), "row"), "rev"
     )
     grad_scale = 1.0 / math.sqrt(lax.axis_size("rev") * KX * KY)
     return (

time: 393 us -> 406 us (1.033)
  blocking collectives: 109 us -> 122 us
    psum x0 -> x1, blocking collectives: none -> 22.9 us  [local(): lax.psum(lax.psum((param_grads[0], param_grads[1], param_grads[2], param_...]
    psum x1, blocking collectives: 57.3 us -> 47.1 us  [local(): lax.psum((param_grads[0], param_grads[1], param_grads[2], param_grads[3])...]
  transfers between devices with their start and end apart: 4 -> 4, of which waited for: 3 -> 3; matrix products, arithmetic and copies ran while one was open for 18% -> 17% of each run, Pallas kernels for 0% -> 0%
where the time goes in v1:
time: 406 us; the launch traced here: 398 us
  blocking collectives  122 us (30%)
  matrix products  93.6 us (23%)
  waiting for transfers between devices  78.3 us (19%)
  local copies, waits for them, and re-layouts  65.6 us (16%)
  starting transfers between devices  19.6 us (5%)
  other arithmetic  15.3 us (4%)
  between operations  4.31 us (1%)
    all_to_all x1, blocking collectives, route(): lax.all_to_all(slot_array, 'rev', split_axis=0, concat_axis=0, tiled=True)  51.6 us
    psum x1, blocking collectives, local(): lax.psum((param_grads[0], param_grads[1], param_grads[2], param_grads[3])...  47.1 us
    all_to_all x1, waiting for transfers between devices, local(): lax.all_to_all(field_cols, 'row', split_axis=3, concat_axis=2, tiled=True)  30.1 us
    all_to_all x1, waiting for transfers between devices, route(): lax.all_to_all(slot_array, 'rev', split_axis=0, concat_axis=0, tiled=True)  26.5 us
    dot_general x20, matrix products, mixing(): return jnp.einsum('bio,bipq->bopq', matrix, values, precision=HIGHEST)  25.2 us
    psum x1, blocking collectives, local(): lax.psum(lax.psum((param_grads[0], param_grads[1], param_grads[2], param_...  22.9 us
    unnamed x51, local copies, waits for them, and re-layouts  22.5 us
    all_to_all x1, waiting for transfers between devices, local(): lax.all_to_all(grad_cols, 'row', split_axis=3, concat_axis=2, tiled=True)  21.7 us
  transfers between devices with their start and end apart: 4, of which 3 were waited for; matrix products, arithmetic and copies ran while one was open for 17% of the time, Pallas kernels for 0%

profile of v1, /device:TPU:0, one launch (start us, length us, event | category | flops | bytes accessed | tf_op | source)
XLA Modules:
  0.0 398.4 jit_solution(2357647858148265642)
XLA Ops:
  0.6 8.1 %fusion.1 = bf16[128,4096]{1,0:T(8,128)(2,1)S(1)} fusion(bf16[4096,1024]{1,0:T(8,128)(2,1)} %bitcast.364), kind=kOutput, calls=%fused_computation.4 | convolution fusion | flops 1076756480 | bytes 9437184 | tf_op jit(solution)/shard_map/dot_general | solution.py:85
  8.8 4.6 %convolution_convert_fusion = bf16[128,4096]{1,0:T(8,128)(2,1)S(1)} fusion(bf16[4096,1024]{1,0:T(8,128)(2,1)S(1)} %bitcast.365), kind=kOutput, calls=%fused_computation.5 | convolution fusion | flops 1076232192 | bytes 9437184 | tf_op jit(solution)/shard_map/dot_general | solution.py:84
  15.4 6.5 %all-to-all-start.1 = ((bf16[2,16,256,128]{2,1,0,3:T(8,128)(2,1)}), bf16[2,16,256,128]{2,1,0,3:T(8,128)(2,1)S(1)}, u32[]{:S(2)}, u32[]{:S(2)}) async-start(bf16[2,16,256,128]{2,1,0,3:T(8,128)(2,1)} %pad_maximum_fusion.1), calls=%async_computation.1 | async-start | bytes 4194304 | tf_op jit(solution)/shard_map/all_to_all | solution.py:124
  21.9 8.0 %fusion = bf16[128,4096]{1,0:T(8,128)(2,1)S(1)} fusion(bf16[4096,1024]{1,0:T(8,128)(2,1)} %bitcast.366), kind=kOutput, calls=%fused_computation.3 | convolution fusion | flops 1076756480 | bytes 9437184 | tf_op jit(solution)/shard_map/dot_general | solution.py:85
  30.2 8.0 %convolution_convert_fusion.1 = bf16[128,4096]{1,0:T(8,128)(2,1)S(1)} fusion(bf16[4096,1024]{1,0:T(8,128)(2,1)} %bitcast.367), kind=kOutput, calls=%fused_computation.6 | convolution fusion | flops 1076232192 | bytes 9437184 | tf_op jit(solution)/shard_map/dot_general | solution.py:84
  40.0 30.1 %all-to-all-done.1 = bf16[2,16,256,128]{2,1,0,3:T(8,128)(2,1)S(1)} async-done(((bf16[2,16,256,128]{2,1,0,3:T(8,128)(2,1)}), bf16[2,16,256,128]{2,1,0,3:T(8,128)(2,1)S(1)}, u32[]{:S(2)}, u32[]{:S(2)}) %all-to-all-start.1) | async-done | bytes 2097184 | tf_op jit(solution)/shard_map/all_to_all | solution.py:124
  71.4 4.0 %all-to-all-start = ((bf16[2,16,256,128]{2,1,0,3:T(8,128)(2,1)}), bf16[2,16,256,128]{2,1,0,3:T(8,128)(2,1)S(1)}, u32[]{:S(2)}, u32[]{:S(2)}) async-start(bf16[2,16,256,128]{2,1,0,3:T(8,128)(2,1)} %pad_maximum_fusion), calls=%async_computation | async-start | bytes 4194304 | tf_op jit(solution)/shard_map/all_to_all | solution.py:127
  78.0 4.5 %copy.142 = bf16[2,16,256,4,32]{2,3,4,1,0:T(4,128)(2,1)} copy(bf16[2,16,256,4,32]{2,1,0,4,3:T(8,128)(2,1)} %bitcast.346) | data formatting | bytes 4194304 | tf_op jit(solution)/shard_map/all_to_all | solution.py:124
  82.5 4.4 %all_to_all.50 = bf16[2,16,1024,32]{2,3,1,0:T(8,128)(2,1)} reshape(bf16[2,16,4,256,32]{3,2,4,1,0:T(4,128)(2,1)} %bitcast.347) | data formatting | bytes 4194304 | tf_op jit(solution)/shard_map/all_to_all | solution.py:124
  87.0 6.3 %fusion.88 = f32[2,16,32,256]{3,2,1,0:T(8,128)S(1)} fusion(bf16[2,16,1024,32]{2,3,1,0:T(8,128)(2,1)} %all_to_all.50, s32[256]{0:T(256)S(1)} %compare_select_fusion.1), kind=kOutput, calls=%fused_computation.150 | convolution fusion | flops 540803072 | bytes 3146752 | tf_op jit(solution)/shard_map/schk,jh->sckj/dot_general | solution.py:91
  93.3 4.5 %fusion.93 = f32[2,16,32,256]{3,2,1,0:T(8,128)S(1)} fusion(bf16[2,16,1024,32]{2,3,1,0:T(8,128)(2,1)S(1)} %copy-done.4, s32[256]{0:T(256)S(1)} %compare_select_fusion.1), kind=kOutput, calls=%fused_computation.152 | convolution fusion | flops 540803072 | bytes 3146752 | tf_op jit(solution)/shard_map/schk,jh->sckj/dot_general | solution.py:90
  98.0 2.5 broadcast.158.clone
  101.4 21.7 %all-to-all-done = bf16[2,16,256,128]{2,1,0,3:T(8,128)(2,1)S(1)} async-done(((bf16[2,16,256,128]{2,1,0,3:T(8,128)(2,1)}), bf16[2,16,256,128]{2,1,0,3:T(8,128)(2,1)S(1)}, u32[]{:S(2)}, u32[]{:S(2)}) %all-to-all-start) | async-done | bytes 2097184 | tf_op jit(solution)/shard_map/all_to_all | solution.py:127
  123.1 4.6 %all-to-all-start.2 = ((bf16[8,2,16,32,256]{4,3,2,1,0:T(8,128)(2,1)}), bf16[8,2,16,32,256]{4,3,2,1,0:T(8,128)(2,1)}, u32[]{:S(2)}, u32[]{:S(2)}) async-start(bf16[8,2,16,32,256]{4,3,2,1,0:T(8,128)(2,1)} %fusion.62), calls=%async_computation.2 | async-start | bytes 8388608 | tf_op jit(solution)/shard_map/all_to_all | solution.py:134
  129.1 3.0 copy.143
  132.0 3.4 all_to_all.46
  136.5 4.5 %fusion.90 = f32[2,16,32,256]{3,2,1,0:T(8,128)S(1)} fusion(bf16[2,16,1024,32]{2,3,1,0:T(8,128)(2,1)S(1)} %all_to_all.46, s32[256]{0:T(256)S(1)} %compare_select_fusion.1), kind=kOutput, calls=%fused_computation.151 | convolution fusion | flops 540803072 | bytes 3146752 | tf_op jit(solution)/shard_map/schk,jh->sckj/dot_general | solution.py:91
  141.1 4.5 %fusion.95 = f32[2,16,32,256]{3,2,1,0:T(8,128)S(1)} fusion(bf16[2,16,1024,32]{2,3,1,0:T(8,128)(2,1)S(1)} %all_to_all.46, s32[256]{0:T(256)S(1)} %compare_select_fusion.1), kind=kOutput, calls=%fused_computation.153 | convolution fusion | flops 540803072 | bytes 3146752 | tf_op jit(solution)/shard_map/schk,jh->sckj/dot_general | solution.py:90
  150.3 26.5 %all-to-all-done.2 = bf16[8,2,16,32,256]{4,3,2,1,0:T(8,128)(2,1)} async-done(((bf16[8,2,16,32,256]{4,3,2,1,0:T(8,128)(2,1)}), bf16[8,2,16,32,256]{4,3,2,1,0:T(8,128)(2,1)}, u32[]{:S(2)}, u32[]{:S(2)}) %all-to-all-start.2) | async-done | bytes 4194336 | tf_op jit(solution)/shard_map/all_to_all | solution.py:134
  191.0 2.5 fusion.28
  194.1 51.6 %all_to_all.61 = bf16[8,2,16,32,256]{4,3,2,1,0:T(8,128)(2,1)S(1)} all-to-all(bf16[8,2,16,32,256]{4,3,2,1,0:T(8,128)(2,1)S(1)} %fusion.64), channel_id=1, replica_groups=mesh['rev'=8,'row'=4] {'rev'}, dimensions={0} | all-to-all | bytes 8388608 | tf_op jit(solution)/shard_map/all_to_all | solution.py:134
  245.8 4.6 %convolution_bitcast_fusion = f32[2,16,1024,32]{2,3,1,0:T(8,128)S(1)} fusion(bf16[2,16,32,256]{3,2,1,0:T(8,128)(2,1)S(1)} %fusion.22, s32[256]{0:T(256)S(1)} %compare_select_fusion.1), kind=kOutput, calls=%fused_computation.7 | convolution fusion | flops 540803072 | bytes 4719616 | tf_op jit(solution)/shard_map/sckj,jh->schk/dot_general | solution.py:99
  250.4 4.5 %convolution_bitcast_fusion.1 = f32[2,16,1024,32]{2,3,1,0:T(8,128)S(1)} fusion(bf16[2,16,32,256]{3,2,1,0:T(8,128)(2,1)S(1)} %fusion.22, s32[256]{0:T(256)S(1)} %compare_select_fusion.1), kind=kOutput, calls=%fused_computation.8 | convolution fusion | flops 540803072 | bytes 4719616 | tf_op jit(solution)/shard_map/sckj,jh->schk/dot_general | solution.py:98
  257.7 12.5 %copy.77 = bf16[2,16,1024,32]{3,1,0,2:T(8,128)(2,1)} copy(bf16[2,16,1024,32]{2,3,1,0:T(8,128)(2,1)} %pad_maximum_fusion.2) | data formatting | bytes 4194304 | tf_op jit(solution)/shard_map/stack | solution.py:102
  270.1 10.7 %reshape.381 = bf16[4,2,131072]{2,1,0:T(2,128)(2,1)} reshape(bf16[1024,2,16,32]{3,2,1,0:T(8,128)(2,1)} %bitcast.340) | data formatting | bytes 4194304
  280.9 4.5 %all-to-all-start.4 = ((bf16[4,2,131072]{2,1,0:T(2,128)(2,1)}), bf16[4,2,131072]{2,1,0:T(2,128)(2,1)}, u32[]{:S(2)}, u32[]{:S(2)}) async-start(bf16[4,2,131072]{2,1,0:T(2,128)(2,1)} %reshape.381), calls=%async_computation.4 | async-start | bytes 4194304 | tf_op jit(solution)/shard_map/all_to_all | solution.py:148
  295.3 47.1 %all-reduce.11 = (f32[1,2,32,16]{2,3,1,0:T(8,128)S(1)}, f32[1,2,16]{2,1,0:T(2,128)S(1)}, f32[1,2,16,16]{2,3,1,0:T(8,128)S(1)}, f32[1,2,16]{2,1,0:T(2,128)S(1)}) all-reduce(f32[1,2,32,16]{2,3,1,0:T(8,128)S(1)} %pad_add_fusion.2, f32[1,2,16]{2,1,0:T(2,128)S(1)} %get-tuple-element.52, ...), channel_id=1, replica_groups=mesh['rev'=8,'row'=4] {'row'}, use_global_device_ids=true, to_apply=%region_0.1 | all-reduce | flops 1600 | bytes 12800 | tf_op jit(solution)/shard_map/psum | solution.py:151
  342.4 22.9 %all-reduce.10 = (f32[1,2,32,16]{2,3,1,0:T(8,128)S(1)}, f32[1,2,16]{2,1,0:T(2,128)S(1)}, f32[1,2,16,16]{2,3,1,0:T(8,128)S(1)}, f32[1,2,16]{2,1,0:T(2,128)S(1)}) all-reduce(f32[1,2,32,16]{2,3,1,0:T(8,128)S(1)} %get-tuple-element.26, f32[1,2,16]{2,1,0:T(2,128)S(1)} %get-tuple-element.27, ...), channel_id=1, replica_groups=mesh['rev'=8,'row'=4] {'rev'}, use_global_device_ids=true, to_apply=%region_1.2 | all-reduce | flops 1600 | bytes 12800 | tf_op jit(solution)/shard_map/psum | solution.py:150
  367.7 7.3 %reshape.382 = bf16[1024,2,16,32]{3,2,1,0:T(8,128)(2,1)} reshape(bf16[4,2,131072]{2,1,0:T(2,128)(2,1)} %all-to-all-done.4) | data formatting | bytes 4194304
  375.1 10.9 %copy.78 = bf16[2,16,4,256,32]{3,1,4,2,0:T(8,128)(2,1)S(1)} copy(bf16[2,16,4,256,32]{4,1,0,3,2:T(8,128)(2,1)} %bitcast.341) | data formatting | bytes 4194304 | tf_op jit(solution)/shard_map/all_to_all | solution.py:148
  387.1 4.4 %fusion.110 = f32[4096,1024]{1,0:T(8,128)S(1)} fusion(bf16[4096,128]{0,1:T(8,128)(2,1)S(1)} %bitcast.349), kind=kOutput, calls=%fused_computation.171 | convolution fusion | flops 1075707904 | bytes 17825792 | tf_op jit(solution)/shard_map/hk,wk->hw/dot_general | solution.py:109
  391.5 6.5 %multiply_convert_fusion = bf16[4096,1024]{1,0:T(8,128)(2,1)} fusion(f32[4096,1024]{1,0:T(8,128)S(1)} %fusion.110, bf16[4096,128]{0,1:T(8,128)(2,1)S(1)} %bitcast.343), kind=kOutput, calls=%fused_computation | convolution fusion | flops 1088290816 | bytes 26214400 | tf_op jit(solution)/shard_map/hk,wk->hw/dot_general | solution.py:110
  (100 shorter events, 44.4 us)
Async XLA Ops:
  0.6 8.1 %copy-start.18 = (bf16[1,16,256,1024]{3,2,1,0:T(8,128)(2,1)S(1)}, bf16[1,16,256,1024]{3,2,1,0:T(8,128)(2,1)}, u32[]{:S(2)}) copy-start(bf16[1,16,256,1024]{3,2,1,0:T(8,128)(2,1)} %param.7) | copy-start | bytes 25165828
  15.4 54.7 %all-to-all-start.1 = ((bf16[2,16,256,128]{2,1,0,3:T(8,128)(2,1)}), bf16[2,16,256,128]{2,1,0,3:T(8,128)(2,1)S(1)}, u32[]{:S(2)}, u32[]{:S(2)}) async-start(bf16[2,16,256,128]{2,1,0,3:T(8,128)(2,1)} %pad_maximum_fusion.1), calls=%async_computation.1 | async-start | bytes 4194304 | tf_op jit(solution)/shard_map/all_to_all | solution.py:124
  40.0 35.5 %copy-start.19 = (s32[8]{0:T(128)S(1)}, s32[8]{0:T(128)}, u32[]{:S(2)}) copy-start(s32[8]{0:T(128)} %param.9) | copy-start | bytes 100
  70.1 1.3 copy-start
  71.4 51.7 %all-to-all-start = ((bf16[2,16,256,128]{2,1,0,3:T(8,128)(2,1)}), bf16[2,16,256,128]{2,1,0,3:T(8,128)(2,1)S(1)}, u32[]{:S(2)}, u32[]{:S(2)}) async-start(bf16[2,16,256,128]{2,1,0,3:T(8,128)(2,1)} %pad_maximum_fusion), calls=%async_computation | async-start | bytes 4194304 | tf_op jit(solution)/shard_map/all_to_all | solution.py:127
  87.0 6.3 %copy-start.4 = (bf16[2,16,1024,32]{2,3,1,0:T(8,128)(2,1)S(1)}, bf16[2,16,1024,32]{2,3,1,0:T(8,128)(2,1)}, u32[]{:S(2)}) copy-start(bf16[2,16,1024,32]{2,3,1,0:T(8,128)(2,1)} %all_to_all.50) | copy-start | bytes 6291460
  101.4 26.3 %copy-start.20 = (s32[8]{0:T(128)S(1)}, s32[8]{0:T(128)}, u32[]{:S(2)}) copy-start(s32[8]{0:T(128)} %param.10) | copy-start | bytes 100
  101.4 27.5 %copy-start.17 = (f32[1,2,16]{2,1,0:T(2,128)S(1)}, f32[1,2,16]{2,1,0:T(2,128)}, u32[]{:S(2)}) copy-start(f32[1,2,16]{2,1,0:T(2,128)} %param.12) | copy-start | bytes 388
  123.1 53.7 %all-to-all-start.2 = ((bf16[8,2,16,32,256]{4,3,2,1,0:T(8,128)(2,1)}), bf16[8,2,16,32,256]{4,3,2,1,0:T(8,128)(2,1)}, u32[]{:S(2)}, u32[]{:S(2)}) async-start(bf16[8,2,16,32,256]{4,3,2,1,0:T(8,128)(2,1)} %fusion.62), calls=%async_computation.2 | async-start | bytes 8388608 | tf_op jit(solution)/shard_map/all_to_all | solution.py:134
  145.8 1.2 copy-start.16
  147.0 1.7 copy-start.1
  147.0 31.0 %copy-start.3 = (f32[2,1,16,32,256]{4,3,2,1,0:T(8,128)S(1)}, f32[2,1,16,32,256]{4,3,2,1,0:T(8,128)}, u32[]{:S(2)}) copy-start(f32[2,1,16,32,256]{4,3,2,1,0:T(8,128)} %maximum_multiply_fusion.1) | copy-start | bytes 3145732
  178.0 0.7 copy-start.15
  180.4 2.6 copy-start.5
  180.4 2.6 copy-start.14
  183.0 2.3 copy-start.9
  185.3 2.3 copy-start.7
  185.3 2.3 copy-start.13
  187.6 2.3 copy-start.11
  280.9 86.9 %all-to-all-start.4 = ((bf16[4,2,131072]{2,1,0:T(2,128)(2,1)}), bf16[4,2,131072]{2,1,0:T(2,128)(2,1)}, u32[]{:S(2)}, u32[]{:S(2)}) async-start(bf16[4,2,131072]{2,1,0:T(2,128)(2,1)} %reshape.381), calls=%async_computation.4 | async-start | bytes 4194304 | tf_op jit(solution)/shard_map/all_to_all | solution.py:148
  286.7 4.3 %copy-start.8 = (f32[16,32,256]{2,1,0:T(8,128)S(1)}, f32[16,32,256]{2,1,0:T(8,128)}, u32[]{:S(2)}) copy-start(f32[16,32,256]{2,1,0:T(8,128)} %get-tuple-element.40) | copy-start | bytes 1572868
  286.7 4.3 %copy-start.12 = (f32[32,256,16]{1,2,0:T(8,128)S(1)}, f32[32,256,16]{1,2,0:T(8,128)}, u32[]{:S(2)}) copy-start(f32[32,256,16]{1,2,0:T(8,128)} %copy-done.11) | copy-start | bytes 1572868
  288.1 3.9 copy-start.6
  288.1 3.9 copy-start.10
  289.5 3.5 copy-start.2
